TPU v7x, 256 devices: a whole 4x4x8 slice. The times are simulated.
256 devices in a mesh: tm: 32 (over y_hi, z, core), head: 4 (over x), rep: 2 (over y_lo).
Axes of the slice: x: 4, y: 4 (y_hi: 2, y_lo: 2; y = y_hi * 2 + y_lo), z: 8, core: 2. Of those that a mesh axis runs over, the one named last changes fastest.
Arguments:
- queries: bfloat16 [32768, 1536], P(('tm', 'rep'), 'head'), may hold values from -8 to 8
- kv_cache: bfloat16 [32768, 2, 1536], P('tm', None, 'head'), may hold values from -8 to 8
- out_weight: bfloat16 [1536, 3072], P('head'), may hold values from -0.15625 to 0.15625
- fetch_list: int32 [64, 32], P(('tm', 'rep')), may hold values from 0 to 247, as said below
- tile_lists: int32 [256, 16], P(('tm', 'rep')), may hold values from 0 to 31, as said below
- event_offsets: int32 [256], P(('tm', 'rep')), may hold values from 0 to 7
Outputs:
- mixed: bfloat16 [32768, 3072], P(('tm', 'rep'), 'head')
Inputs may be any that keep to these rules, and one draw needn't show every extreme that they name: `fetch_list`: each row names 32 distinct blocks, all with ids below (31) * 8, so none of the newest ones; one row names at most 2 blocks of one owner, and every row names exactly 2 blocks of some owner. `tile_lists`: each row names 16 distinct positions; the tiles of one device together name every position of its row of fetch_list.
All inputs are finite; a program needn't handle non-finite values.
Results may differ from a plain program's by a relative error of at most 0.013.
Values may be sent and summed in bfloat16 or wider, within the bound.
No kernel may reach another device: no remote copies, remote signals or barrier semaphores. Data moves between devices by JAX's collectives and lax.ppermute only.
A program may use at most 128 MiB of HBM per device.

v0:
```python
import math
import jax
import jax.numpy as jnp
from jax import lax
from jax.sharding import PartitionSpec as P

DH = 128
TILE = 128
CB_DEV = 8
CAP = 2


def from_root(shard, axis, root):
    mine = lax.axis_index(axis) == root
    return lax.psum(jnp.where(mine, shard, jnp.zeros_like(shard)), axis)


def owner_ranks(owners):
    entry_count = owners.shape[-1]
    index_row = jnp.arange(entry_count, dtype=jnp.int32)
    same_owner = owners[..., None, :] == owners[..., :, None]
    earlier = index_row[None, :] < index_row[:, None]
    return jnp.sum(same_owner & earlier, axis=-1)


def outgoing(requests, wanted, block_rows, me_owner):
    owners = requests // CB_DEV
    slot_ids = requests % CB_DEV
    rank_ids = owner_ranks(owners)
    is_mine = owners == me_owner
    hit_table = is_mine[:, :, None] & (rank_ids[:, :, None] == wanted[None, None, :])
    chosen = jnp.sum(jnp.where(hit_table, slot_ids[:, :, None], 0), axis=1)
    in_use = jnp.any(hit_table, axis=1)
    picked = jnp.take(block_rows, chosen, axis=0)
    return jnp.where(in_use[:, :, None, None, None], picked, jnp.zeros_like(picked))


def shards(queries, kv_cache, out_weight, fetch_list, tile_lists, event_offsets):
    me_owner = lax.axis_index("tm")
    feature_width = kv_cache.shape[2]
    head_count = feature_width // DH
    block_rows = kv_cache.reshape(CB_DEV, -1, 2, feature_width)
    block_len = block_rows.shape[1]
    own_owners = fetch_list[0] // CB_DEV
    own_ranks = owner_ranks(own_owners)
    requests = lax.all_gather(fetch_list, "tm", axis=0, tiled=True)
    outbound = outgoing(requests, jnp.arange(CAP, dtype=jnp.int32), block_rows, me_owner)
    arrived = lax.all_to_all(outbound, "tm", split_axis=0, concat_axis=0, tiled=True)
    flat_blocks = arrived.reshape(-1, block_len, 2, feature_width)
    fetched = jnp.take(flat_blocks, own_owners * CAP + own_ranks, axis=0)
    newest = lax.axis_size("tm") - 1
    panel_rows = from_root(kv_cache, "tm", newest)
    panel_keys = panel_rows[:, 0].reshape(-1, head_count, DH)
    panel_values = panel_rows[:, 1].reshape(-1, head_count, DH)
    slab_rows = panel_keys.shape[0]
    tile_count = queries.shape[0] // TILE
    per_step = math.gcd(tile_count, 4)
    query_groups = queries.reshape(tile_count // per_step, per_step, TILE, head_count, DH)
    list_groups = tile_lists.reshape(tile_count // per_step, per_step, -1)
    offset_groups = event_offsets.reshape(tile_count // per_step, per_step)
    score_scale = 1.0 / math.sqrt(DH)
    positions = jnp.arange(slab_rows, dtype=jnp.int32)

    def attend(pieces):
        query_block, list_rows, offsets = pieces
        picked = jnp.take(fetched, list_rows, axis=0).reshape(per_step, -1, 2, feature_width)
        far_keys = picked[:, :, 0].reshape(per_step, -1, head_count, DH)
        far_values = picked[:, :, 1].reshape(per_step, -1, head_count, DH)
        far_scores = (
            jnp.einsum("gqhd,gkhd->ghqk", query_block, far_keys, preferred_element_type=jnp.float32)
            * score_scale
        )
        near_scores = (
            jnp.einsum(
                "gqhd,khd->ghqk", query_block, panel_keys, preferred_element_type=jnp.float32
            )
            * score_scale
        )
        visible = positions[None, :] < (CB_DEV - offsets)[:, None] * block_len
        near_scores = jnp.where(visible[:, None, None, :], near_scores, -1e30)
        row_max = jnp.maximum(jnp.max(far_scores, axis=-1), jnp.max(near_scores, axis=-1))
        far_weights = jnp.exp(far_scores - row_max[..., None])
        near_weights = jnp.exp(near_scores - row_max[..., None])
        denom_sum = jnp.sum(far_weights, axis=-1) + jnp.sum(near_weights, axis=-1)
        blended = jnp.einsum(
            "ghqk,gkhd->gqhd",
            far_weights.astype(jnp.bfloat16),
            far_values,
            preferred_element_type=jnp.float32,
        )
        blended = blended + jnp.einsum(
            "ghqk,khd->gqhd",
            near_weights.astype(jnp.bfloat16),
            panel_values,
            preferred_element_type=jnp.float32,
        )
        blended = blended / jnp.transpose(denom_sum, (0, 2, 1))[..., None]
        return blended.astype(jnp.bfloat16).reshape(per_step, TILE, head_count * DH)

    attended = lax.map(attend, (query_groups, list_groups, offset_groups)).reshape(
        -1, head_count * DH
    )
    partial_value = jnp.dot(attended, out_weight, preferred_element_type=jnp.float32)
    return lax.psum_scatter(
        partial_value.astype(jnp.bfloat16), "head", scatter_dimension=1, tiled=True
    )


def solution(mesh):
    placed = (
        P(("tm", "rep"), "head"),
        P("tm", None, "head"),
        P("head", None),
        P(("tm", "rep"), None),
        P(("tm", "rep"), None),
        P(("tm", "rep")),
    )
    return jax.shard_map(
        shards, mesh=mesh, in_specs=placed, out_specs=P(("tm", "rep"), "head"), check_vma=False
    )
```

profile of v0, /device:TPU:1, one launch (start us, length us, event | category | flops | bytes accessed | tf_op | source)
XLA Modules:
  0.0 600.0 jit_solution(15882582718426881978)
XLA Ops:
  6.5 46.3 %all-gather = s32[32,1,32]{2,1,0:T(1,128)S(1)} all-gather(s32[1,1,32]{2,1,0:T(1,128)} %bitcast.112), channel_id=1, replica_groups=mesh['tm'=32,'head'=4,'rep'=2] {'tm'}, dimensions={0}, use_global_device_ids=true | all-gather | bytes 4224 | tf_op jit(solution)/shard_map/all_gather | solution.py:46
  52.9 0.8 convert_reduce_fusion
  53.6 0.1 select_reduce_fusion
  54.1 29.4 %gather_fusion = bf16[64,128,2,384]{3,2,1,0:T(2,128)(2,1)} fusion(bf16[8,128,2,384]{3,2,1,0:T(2,128)(2,1)} %bitcast.101, s32[1024]{0:T(1024)S(1)} %pad_clamp_fusion.2), kind=kCustom, calls=%fused_computation | custom fusion | bytes 25166080 | tf_op jit(solution)/shard_map/jit(_take)/gather | solution.py:34
  83.5 11.5 %copy.119 = bf16[64,128,2,384]{3,1,2,0:T(8,128)(2,1)} copy(bf16[64,128,2,384]{3,2,1,0:T(2,128)(2,1)} %gather_fusion) | data formatting | bytes 25165824 | tf_op jit(solution)/shard_map/jit(_take)/gather | solution.py:34
  95.3 11.0 %select_select_fusion = bf16[32,2,128,2,384]{4,2,3,1,0:T(8,128)(2,1)} fusion(bf16[32,2,128,2,384]{4,2,3,1,0:T(8,128)(2,1)} %bitcast.102, pred[32,2]{1,0:T(8,128)(4,1)S(1)} %copy.117, pred[32,2]{1,0:T(8,128)(4,1)S(1)} %copy.116), kind=kLoop, calls=%fused_computation.7 | loop fusion | flops 12582912 | bytes 25165952 | tf_op jit(solution)/shard_map/jit(_where)/select_n | solution.py:35
  106.3 4.8 all-to-all-start
  111.3 5.0 copy.126
  116.3 1.3 broadcast_select_fusion.1
  117.8 0.2 copy.123
  118.2 0.2 convert_reduce_fusion.1
  118.4 0.6 pad_clamp_fusion.1
  119.0 0.6 compare_and_fusion.1
  119.7 346.7 %all-reduce.2.cloned.1.call-done = bf16[1024,2,384]{0,2,1:T(8,128)(2,1)} async-done(((bf16[1024,2,384]{0,2,1:T(8,128)(2,1)}), bf16[1024,2,384]{0,2,1:T(8,128)(2,1)}) %all-reduce.2.cloned.1.call-update) | async-done | bytes 1572880 | tf_op jit(solution)/shard_map/psum | solution.py:15
  466.4 1.5 fusion.42
  467.9 4.3 fusion.9
  472.2 8.7 %gather_fusion.1 = bf16[32,128,2,384]{3,1,2,0:T(8,128)(2,1)} fusion(bf16[64,128,2,384]{3,1,2,0:T(8,128)(2,1)} %bitcast.7, s32[1024]{0:T(1024)} %pad_clamp_fusion.1), kind=kCustom, calls=%fused_computation.1 | custom fusion | bytes 12583040 | tf_op jit(solution)/shard_map/jit(_take)/gather | solution.py:50
  480.9 6.2 %broadcast_select_fusion = bf16[32,128,2,384]{3,1,2,0:T(8,128)(2,1)} fusion(bf16[32,128,2,384]{3,1,2,0:T(8,128)(2,1)} %gather_fusion.1, pred[32]{0:T(512)(128)(4,1)} %compare_and_fusion.1), kind=kLoop, calls=%fused_computation.15 | loop fusion | flops 3145728 | bytes 12582944 | tf_op jit(solution)/shard_map/jit(_take)/select_n | solution.py:50
  487.1 9.9 %gather_fusion.2 = bf16[64,128,2,384]{3,1,2,0:T(8,128)(2,1)} fusion(bf16[32,128,2,384]{3,1,2,0:T(8,128)(2,1)} %broadcast_select_fusion, s32[1024]{0:T(1024)S(1)} %pad_clamp_fusion), kind=kCustom, calls=%fused_computation.2 | custom fusion | bytes 25166080 | tf_op jit(solution)/shard_map/while/body/eval_jaxpr/jit(_take)/gather | solution.py:66
  496.9 7.0 %copy.120 = bf16[64,128,2,384]{3,1,0,2:T(8,128)(2,1)S(1)} copy(bf16[64,128,2,384]{3,1,2,0:T(8,128)(2,1)} %gather_fusion.2) | data formatting | bytes 25165824 | tf_op jit(solution)/shard_map/while/body/eval_jaxpr/jit(_take)/gather | solution.py:66
  504.0 3.0 bitcast_select_fusion
  506.9 5.7 fusion.41
  512.7 8.7 %copy.121 = bf16[4,2048,1,384]{1,3,0,2:T(8,128)(2,1)} copy(bf16[4,2048,1,384]{3,1,0,2:T(8,128)(2,1)} %get-tuple-element.24) | data formatting | bytes 12582912 | tf_op jit(solution)/shard_map/while/body/eval_jaxpr/slice | solution.py:68
  521.3 8.6 %copy.122 = bf16[4,2048,1,384]{1,3,0,2:T(8,128)(2,1)} copy(bf16[4,2048,1,384]{3,1,0,2:T(8,128)(2,1)} %get-tuple-element.23) | data formatting | bytes 12582912 | tf_op jit(solution)/shard_map/while/body/eval_jaxpr/slice | solution.py:67
  529.9 4.7 bitcast_reduce_fusion
  534.6 2.1 fusion.1
  536.7 5.4 fusion.12
  542.1 4.7 fusion.7
  546.9 0.6 fusion.24
  547.5 0.3 copy.134
  547.9 3.5 convolution_convert_fusion
  551.4 41.8 %reduce-scatter.2.cloned.1.call-done = bf16[512,768]{1,0:T(8,128)(2,1)} async-done(((bf16[512,3072]{1,0:T(8,128)(2,1)}), bf16[512,768]{1,0:T(8,128)(2,1)}) %reduce-scatter.2.cloned.1.call-update) | async-done | bytes 786448 | tf_op jit(solution)/shard_map/reduce_scatter | solution.py:104
  (43 shorter events, 1.1 us)
Async XLA Ops:
  6.5 541.3 %copy-start = (bf16[384,3072]{1,0:T(8,128)(2,1)S(1)}, bf16[384,3072]{1,0:T(8,128)(2,1)}, u32[]{:S(2)}) copy-start(bf16[384,3072]{1,0:T(8,128)(2,1)} %param.8) | copy-start | bytes 7077892
  106.3 365.9 %all-to-all-start = ((bf16[32,2,128,2,384]{4,2,3,1,0:T(8,128)(2,1)}), bf16[32,2,128,2,384]{4,2,3,1,0:T(8,128)(2,1)}, u32[]{:S(2)}, u32[]{:S(2)}) async-start(bf16[32,2,128,2,384]{4,2,3,1,0:T(8,128)(2,1)} %select_select_fusion), calls=%async_computation | async-start | bytes 25165824 | tf_op jit(solution)/shard_map/all_to_all | solution.py:48
  111.2 6.5 %copy-start.3 = (s32[4,16]{1,0:T(4,128)S(1)}, s32[4,16]{1,0:T(4,128)}, u32[]{:S(2)}) copy-start(s32[4,16]{1,0:T(4,128)} %param.10) | copy-start | bytes 772
  111.2 6.7 %copy-start.1 = (bf16[512,384]{1,0:T(8,128)(2,1)S(1)}, bf16[512,384]{1,0:T(8,128)(2,1)}, u32[]{:S(2)}) copy-start(bf16[512,384]{1,0:T(8,128)(2,1)} %param.6) | copy-start | bytes 1179652
  111.2 7.0 %copy-start.4 = (s32[1,32]{1,0:T(1,128)S(1)}, s32[1,32]{1,0:T(1,128)}, u32[]{:S(2)}) copy-start(s32[1,32]{1,0:T(1,128)} %param.9) | copy-start | bytes 388
  111.2 7.8 %copy-start.5 = (s32[4]{0:T(128)S(1)}, s32[4]{0:T(128)}, u32[]{:S(2)}) copy-start(s32[4]{0:T(128)} %param.11) | copy-start | bytes 52
  111.2 355.2 %all-reduce.2.cloned.1.call-start = ((), (), s32[]{:S(2)}) async-start(), calls=%async_computation.2 | async-start | bytes 3145728 | tf_op jit(solution)/shard_map/psum | solution.py:15
  117.6 475.6 %reduce-scatter.2.cloned.1.call-start = ((), (), s32[]{:S(2)}) async-start(), calls=%async_computation.3 | async-start | bytes 3932160 | tf_op jit(solution)/shard_map/reduce_scatter | solution.py:104
  529.9 4.7 copy-start.2
Sparse Core Ops, SparseCore 0:
  117.7 348.6 all-reduce.1
  551.5 41.6 reduce-scatter.1
where the time goes:
time: 601 us; the launch traced here: 600 us
  waiting for transfers between devices  389 us (65%)
  local copies, waits for them, and re-layouts  97.3 us (16%)
  blocking collectives  46.3 us (8%)
  other arithmetic  30.8 us (5%)
  matrix products  18.6 us (3%)
  between operations  13.7 us (2%)
    psum x1, waiting for transfers between devices, from_root(): return lax.psum(jnp.where(mine, shard, jnp.zeros_like(shard)), axis)  347 us
    all_gather x1, blocking collectives, shards(): requests = lax.all_gather(fetch_list, 'tm', axis=0, tiled=True)  46.3 us
    reduce_scatter x1, waiting for transfers between devices, shards(): lax.psum_scatter(partial_value.astype(jnp.bfloat16), 'head', scatter_dime...  41.8 us
    gather x2, local copies, waits for them, and re-layouts, outgoing(): picked = jnp.take(block_rows, chosen, axis=0)  40.9 us
    gather x2, local copies, waits for them, and re-layouts, attend(): jnp.take(fetched, list_rows, axis=0).reshape(per_step, -1, 2, feature_width)  16.9 us
    slice x2, local copies, waits for them, and re-layouts, attend(): far_keys = picked[:, :, 0].reshape(per_step, -1, head_count, DH)  14.3 us
  transfers between devices with their start and end apart: 3, of which 2 were waited for; matrix products, arithmetic and copies ran while one was open for 2% of the time, Pallas kernels for 0%

commit v1 on v0

--- a/solution.py
+++ b/solution.py
@@ -3,6 +3,7 @@
 import jax.numpy as jnp
 from jax import lax
 from jax.sharding import PartitionSpec as P
+from jax.lax import all_to_all, psum
 
 DH = 128
 TILE = 128
@@ -43,7 +44,16 @@
     block_len = block_rows.shape[1]
     own_owners = fetch_list[0] // CB_DEV
     own_ranks = owner_ranks(own_owners)
-    requests = lax.all_gather(fetch_list, "tm", axis=0, tiled=True)
+
+    def handle_points(unit, axis_key):
+        return jnp.concatenate(
+            all_to_all(
+                jnp.stack(tuple((unit for _ in range(psum(1, axis_key)))), axis=0), axis_key, 0, 0
+            ),
+            0,
+        )
+
+    requests = handle_points(fetch_list, "tm")
     outbound = outgoing(requests, jnp.arange(CAP, dtype=jnp.int32), block_rows, me_owner)
     arrived = lax.all_to_all(outbound, "tm", split_axis=0, concat_axis=0, tiled=True)
     flat_blocks = arrived.reshape(-1, block_len, 2, feature_width)

time: 601 us -> 579 us (0.963)
  blocking collectives: 46.3 us -> 0 us
  starting transfers between devices: 4.92 us -> 18 us
  waiting for transfers between devices: 389 us -> 398 us
    all_gather x1 -> x0, blocking collectives: 46.3 us -> none  [shards(): requests = lax.all_gather(fetch_list, 'tm', axis=0, tiled=True)]
    all_to_all x0 -> x1, starting transfers between devices: none -> 12.8 us  [handle_points(): all_to_all(jnp.stack(tuple((unit for _ in range(psum(1, axis_key)))), axi...]
    all_to_all x0 -> x1, waiting for transfers between devices: none -> 9.25 us  [handle_points(): all_to_all(jnp.stack(tuple((unit for _ in range(psum(1, axis_key)))), axi...]
  transfers between devices with their start and end apart: 3 -> 4, of which waited for: 2 -> 3; matrix products, arithmetic and copies ran while one was open for 2% -> 2% of each run, Pallas kernels for 0% -> 0%
where the time goes in v1:
time: 579 us; the launch traced here: 578 us
  waiting for transfers between devices  398 us (69%)
  local copies, waits for them, and re-layouts  98.7 us (17%)
  other arithmetic  30.9 us (5%)
  matrix products  18.6 us (3%)
  starting transfers between devices  18 us (3%)
  between operations  13.7 us (2%)
    psum x1, waiting for transfers between devices, from_root(): return lax.psum(jnp.where(mine, shard, jnp.zeros_like(shard)), axis)  348 us
    gather x2, local copies, waits for them, and re-layouts, outgoing(): picked = jnp.take(block_rows, chosen, axis=0)  40.9 us
    reduce_scatter x1, waiting for transfers between devices, shards(): lax.psum_scatter(partial_value.astype(jnp.bfloat16), 'head', scatter_dime...  40.6 us
    gather x2, local copies, waits for them, and re-layouts, attend(): jnp.take(fetched, list_rows, axis=0).reshape(per_step, -1, 2, feature_width)  16.9 us
    slice x2, local copies, waits for them, and re-layouts, attend(): far_keys = picked[:, :, 0].reshape(per_step, -1, head_count, DH)  14.3 us
    all_to_all x1, starting transfers between devices, handle_points(): all_to_all(jnp.stack(tuple((unit for _ in range(psum(1, axis_key)))), axi...  12.8 us
  transfers between devices with their start and end apart: 4, of which 3 were waited for; matrix products, arithmetic and copies ran while one was open for 2% of the time, Pallas kernels for 0%

profile of v1, /device:TPU:1, one launch (start us, length us, event | category | flops | bytes accessed | tf_op | source)
XLA Modules:
  0.0 577.9 jit_solution(4613395941587107165)
XLA Ops:
  6.5 1.4 stack.2
  8.0 12.8 %all-to-all-start = ((s32[32,1,32]{2,1,0:T(1,128)}), s32[32,1,32]{2,1,0:T(1,128)S(1)}, u32[]{:S(2)}, u32[]{:S(2)}) async-start(s32[32,1,32]{2,1,0:T(1,128)} %stack.2), calls=%async_computation | async-start | bytes 32768 | tf_op jit(solution)/shard_map/all_to_all | solution.py:50
  20.7 9.3 %all-to-all-done = s32[32,1,32]{2,1,0:T(1,128)S(1)} async-done(((s32[32,1,32]{2,1,0:T(1,128)}), s32[32,1,32]{2,1,0:T(1,128)S(1)}, u32[]{:S(2)}, u32[]{:S(2)}) %all-to-all-start) | async-done | bytes 4128 | tf_op jit(solution)/shard_map/all_to_all | solution.py:50
  30.1 0.8 convert_reduce_fusion
  31.4 29.4 %gather_fusion = bf16[64,128,2,384]{3,2,1,0:T(2,128)(2,1)} fusion(bf16[8,128,2,384]{3,2,1,0:T(2,128)(2,1)} %bitcast.95, s32[1024]{0:T(1024)S(1)} %pad_clamp_fusion.2), kind=kCustom, calls=%fused_computation | custom fusion | bytes 25166080 | tf_op jit(solution)/shard_map/jit(_take)/gather | solution.py:35
  60.8 11.5 %copy.138 = bf16[64,128,2,384]{3,1,2,0:T(8,128)(2,1)} copy(bf16[64,128,2,384]{3,2,1,0:T(2,128)(2,1)} %gather_fusion) | data formatting | bytes 25165824 | tf_op jit(solution)/shard_map/jit(_take)/gather | solution.py:35
  72.5 11.0 %select_select_fusion = bf16[32,2,128,2,384]{4,2,3,1,0:T(8,128)(2,1)} fusion(bf16[32,2,128,2,384]{4,2,3,1,0:T(8,128)(2,1)} %bitcast.96, pred[32,2]{1,0:T(8,128)(4,1)S(1)} %copy.136, pred[32,2]{1,0:T(8,128)(4,1)S(1)} %copy.135), kind=kLoop, calls=%fused_computation.7 | loop fusion | flops 12582912 | bytes 25165952 | tf_op jit(solution)/shard_map/jit(_where)/select_n | solution.py:36
  83.6 5.2 all-to-all-start.1
  88.9 5.0 copy.145
  93.9 1.3 broadcast_select_fusion.1
  95.5 0.2 copy.142
  96.0 0.6 pad_clamp_fusion.1
  96.6 0.6 compare_and_fusion.1
  97.3 348.2 %all-reduce.2.cloned.1.call-done = bf16[1024,2,384]{0,2,1:T(8,128)(2,1)} async-done(((bf16[1024,2,384]{0,2,1:T(8,128)(2,1)}), bf16[1024,2,384]{0,2,1:T(8,128)(2,1)}) %all-reduce.2.cloned.1.call-update) | async-done | bytes 1572880 | tf_op jit(solution)/shard_map/psum | solution.py:16
  445.4 1.5 fusion.42
  446.9 4.3 fusion.9
  451.2 8.7 %gather_fusion.1 = bf16[32,128,2,384]{3,1,2,0:T(8,128)(2,1)} fusion(bf16[64,128,2,384]{3,1,2,0:T(8,128)(2,1)} %bitcast.7, s32[1024]{0:T(1024)} %pad_clamp_fusion.1), kind=kCustom, calls=%fused_computation.1 | custom fusion | bytes 12583040 | tf_op jit(solution)/shard_map/jit(_take)/gather | solution.py:60
  460.0 6.2 %broadcast_select_fusion = bf16[32,128,2,384]{3,1,2,0:T(8,128)(2,1)} fusion(bf16[32,128,2,384]{3,1,2,0:T(8,128)(2,1)} %gather_fusion.1, pred[32]{0:T(512)(128)(4,1)} %compare_and_fusion.1), kind=kLoop, calls=%fused_computation.15 | loop fusion | flops 3145728 | bytes 12582944 | tf_op jit(solution)/shard_map/jit(_take)/select_n | solution.py:60
  466.1 9.9 %gather_fusion.2 = bf16[64,128,2,384]{3,1,2,0:T(8,128)(2,1)} fusion(bf16[32,128,2,384]{3,1,2,0:T(8,128)(2,1)} %broadcast_select_fusion, s32[1024]{0:T(1024)S(1)} %pad_clamp_fusion), kind=kCustom, calls=%fused_computation.2 | custom fusion | bytes 25166080 | tf_op jit(solution)/shard_map/while/body/eval_jaxpr/jit(_take)/gather | solution.py:76
  476.0 7.0 %copy.139 = bf16[64,128,2,384]{3,1,0,2:T(8,128)(2,1)S(1)} copy(bf16[64,128,2,384]{3,1,2,0:T(8,128)(2,1)} %gather_fusion.2) | data formatting | bytes 25165824 | tf_op jit(solution)/shard_map/while/body/eval_jaxpr/jit(_take)/gather | solution.py:76
  483.0 3.0 bitcast_select_fusion
  486.0 5.7 fusion.41
  491.7 8.7 %copy.140 = bf16[4,2048,1,384]{1,3,0,2:T(8,128)(2,1)} copy(bf16[4,2048,1,384]{3,1,0,2:T(8,128)(2,1)} %get-tuple-element.24) | data formatting | bytes 12582912 | tf_op jit(solution)/shard_map/while/body/eval_jaxpr/slice | solution.py:78
  500.4 8.6 %copy.141 = bf16[4,2048,1,384]{1,3,0,2:T(8,128)(2,1)} copy(bf16[4,2048,1,384]{3,1,0,2:T(8,128)(2,1)} %get-tuple-element.23) | data formatting | bytes 12582912 | tf_op jit(solution)/shard_map/while/body/eval_jaxpr/slice | solution.py:77
  509.0 4.7 bitcast_reduce_fusion
  513.7 2.1 fusion.1
  515.8 5.4 fusion.12
  521.2 4.7 fusion.7
  526.0 0.6 fusion.24
  526.6 0.3 copy.153
  526.9 3.5 convolution_convert_fusion
  530.5 40.6 %reduce-scatter.2.cloned.1.call-done = bf16[512,768]{1,0:T(8,128)(2,1)} async-done(((bf16[512,3072]{1,0:T(8,128)(2,1)}), bf16[512,768]{1,0:T(8,128)(2,1)}) %reduce-scatter.2.cloned.1.call-update) | async-done | bytes 786448 | tf_op jit(solution)/shard_map/reduce_scatter | solution.py:114
  (46 shorter events, 1.5 us)
Async XLA Ops:
  6.5 520.4 %copy-start = (bf16[384,3072]{1,0:T(8,128)(2,1)S(1)}, bf16[384,3072]{1,0:T(8,128)(2,1)}, u32[]{:S(2)}) copy-start(bf16[384,3072]{1,0:T(8,128)(2,1)} %param.8) | copy-start | bytes 7077892
  8.0 22.0 %all-to-all-start = ((s32[32,1,32]{2,1,0:T(1,128)}), s32[32,1,32]{2,1,0:T(1,128)S(1)}, u32[]{:S(2)}, u32[]{:S(2)}) async-start(s32[32,1,32]{2,1,0:T(1,128)} %stack.2), calls=%async_computation | async-start | bytes 32768 | tf_op jit(solution)/shard_map/all_to_all | solution.py:50
  83.6 367.7 %all-to-all-start.1 = ((bf16[32,2,128,2,384]{4,2,3,1,0:T(8,128)(2,1)}), bf16[32,2,128,2,384]{4,2,3,1,0:T(8,128)(2,1)}, u32[]{:S(2)}, u32[]{:S(2)}) async-start(bf16[32,2,128,2,384]{4,2,3,1,0:T(8,128)(2,1)} %select_select_fusion), calls=%async_computation.1 | async-start | bytes 25165824 | tf_op jit(solution)/shard_map/all_to_all | solution.py:58
  88.8 6.5 %copy-start.3 = (s32[4,16]{1,0:T(4,128)S(1)}, s32[4,16]{1,0:T(4,128)}, u32[]{:S(2)}) copy-start(s32[4,16]{1,0:T(4,128)} %param.10) | copy-start | bytes 772
  88.8 6.7 %copy-start.1 = (bf16[512,384]{1,0:T(8,128)(2,1)S(1)}, bf16[512,384]{1,0:T(8,128)(2,1)}, u32[]{:S(2)}) copy-start(bf16[512,384]{1,0:T(8,128)(2,1)} %param.6) | copy-start | bytes 1179652
  88.8 7.0 %copy-start.4 = (s32[1,32]{1,0:T(1,128)S(1)}, s32[1,32]{1,0:T(1,128)}, u32[]{:S(2)}) copy-start(s32[1,32]{1,0:T(1,128)} %param.9) | copy-start | bytes 388
  88.8 7.8 %copy-start.5 = (s32[4]{0:T(128)S(1)}, s32[4]{0:T(128)}, u32[]{:S(2)}) copy-start(s32[4]{0:T(128)} %param.11) | copy-start | bytes 52
  88.8 356.6 %all-reduce.2.cloned.1.call-start = ((), (), s32[]{:S(2)}) async-start(), calls=%async_computation.3 | async-start | bytes 3145728 | tf_op jit(solution)/shard_map/psum | solution.py:16
  95.2 475.8 %reduce-scatter.2.cloned.1.call-start = ((), (), s32[]{:S(2)}) async-start(), calls=%async_computation.4 | async-start | bytes 3932160 | tf_op jit(solution)/shard_map/reduce_scatter | solution.py:114
  509.0 4.7 copy-start.2
Sparse Core Ops, SparseCore 0:
  95.3 350.0 all-reduce.1
  530.6 40.3 reduce-scatter.1
